TPU v7x, 256 devices: a whole 4x4x8 slice. The times are simulated.
256 devices in a mesh: orb: 8 (over x, core), dom: 32 (over y, z).
Axes of the slice: x: 4, y: 4, z: 8, core: 2. Of those that a mesh axis runs over, the one named last changes fastest.
Arguments:
- orbitals: float32 [768, 128, 8, 128], P('orb', 'dom'), may hold values from -6 to 6
- potential: float32 [128, 8, 128], P('dom'), may hold values from -1 to 3
- prev_gradient: float32 [768, 128, 8, 128], P('orb', 'dom'), may hold values from -24 to 24
- prev_direction: float32 [768, 128, 8, 128], P('orb', 'dom'), may hold values from -24 to 24
Outputs:
- new_orbitals: float32 [768, 128, 8, 128], P('orb', 'dom')
- new_direction: float32 [768, 128, 8, 128], P('orb', 'dom')
- gradient: float32 [768, 128, 8, 128], P('orb', 'dom')
All inputs are finite; a program needn't handle non-finite values.
Results may differ from a plain program's by a relative error of at most 0.0002.
Values sent between devices are 32-bit elements; how exact they have to be, the bound alone decides.
No kernel may reach another device: no remote copies, remote signals or barrier semaphores. Data moves between devices by JAX's collectives and lax.ppermute only.
A program may use at most 128 MiB of HBM per device.

v0:
```python
import jax
import jax.numpy as jnp
from jax import lax
from jax.sharding import PartitionSpec as P

coeffs = (-205.0 / 72.0, 8.0 / 5.0, -1.0 / 5.0, 8.0 / 315.0, -1.0 / 560.0)
step_length = 0.05


def padded_2(cells, sides, width):
    for axis, dim in sides:
        count = lax.axis_size(axis)
        ends = count - 1
        head = lax.slice_in_dim(cells, 0, width, axis=dim)
        tail = lax.slice_in_dim(cells, cells.shape[dim] - width, cells.shape[dim], axis=dim)
        cells = jnp.concatenate(
            [
                lax.ppermute(tail, axis, [(i, (i + 1) % count) for i in range(ends)]),
                cells,
                lax.ppermute(head, axis, [((i + 1) % count, i) for i in range(ends)]),
            ],
            axis=dim,
        )
    return cells


def laplace(padded, planes, lines, columns):
    center = padded[:, 4 : 4 + planes, 4 : 4 + lines, 4 : 4 + columns]
    total = 3.0 * coeffs[0] * center
    for offset in range(1, 5):
        total = total + coeffs[offset] * (
            padded[:, 4 + offset : 4 + offset + planes, 4 : 4 + lines, 4 : 4 + columns]
            + padded[:, 4 - offset : 4 - offset + planes, 4 : 4 + lines, 4 : 4 + columns]
        )
        total = total + coeffs[offset] * (
            padded[:, 4 : 4 + planes, 4 + offset : 4 + offset + lines, 4 : 4 + columns]
            + padded[:, 4 : 4 + planes, 4 - offset : 4 - offset + lines, 4 : 4 + columns]
        )
        total = total + coeffs[offset] * (
            padded[:, 4 : 4 + planes, 4 : 4 + lines, 4 + offset : 4 + offset + columns]
            + padded[:, 4 : 4 + planes, 4 : 4 + lines, 4 - offset : 4 - offset + columns]
        )
    return total


def highdot(left, right):
    return jnp.dot(left, right, precision=lax.Precision.HIGHEST, preferred_element_type=jnp.float32)


def on_device(orbitals, potential, prev_gradient, prev_direction):
    block = orbitals.shape[0]
    extended = padded_2(orbitals, (("dom", 1),), 4)
    padded = jnp.pad(extended, ((0, 0), (0, 0), (4, 4), (4, 4)))
    lap = laplace(padded, orbitals.shape[1], orbitals.shape[2], orbitals.shape[3])
    image = -0.5 * lap + potential[None] * orbitals
    cmat = orbitals.reshape(block, -1)
    hmat_rows = image.reshape(block, -1)
    cells = cmat.shape[1] * lax.axis_size("dom")
    cell_orbs, cell_images = (
        lax.all_to_all(cmat, "orb", split_axis=1, concat_axis=0, tiled=True),
        lax.all_to_all(hmat_rows, "orb", split_axis=1, concat_axis=0, tiled=True),
    )
    correlation, hamilton = lax.psum(
        (highdot(cell_orbs, cell_orbs.T), highdot(cell_orbs, cell_images.T)), ("orb", "dom")
    )
    correlation = correlation / cells
    hamilton = hamilton / cells
    cell_grad = (
        4.0 * cell_images
        - 2.0 * highdot(correlation.T, cell_images)
        - 2.0 * highdot(hamilton.T, cell_orbs)
    )
    grad = lax.all_to_all(cell_grad, "orb", split_axis=0, concat_axis=1, tiled=True)
    grad = grad.reshape(orbitals.shape)
    both, cross, before = lax.psum(
        (
            jnp.sum(grad * grad),
            jnp.sum(grad * prev_gradient),
            jnp.sum(prev_gradient * prev_gradient),
        ),
        ("orb", "dom"),
    )
    beta = (both - cross) / before
    direction = -grad + beta * prev_direction
    return (orbitals + step_length * direction, direction, grad)


def solution(mesh):
    in_specs = (
        P("orb", "dom", None, None),
        P("dom", None, None),
        P("orb", "dom", None, None),
        P("orb", "dom", None, None),
    )
    out_specs = (
        P("orb", "dom", None, None),
        P("orb", "dom", None, None),
        P("orb", "dom", None, None),
    )
    return jax.shard_map(
        on_device, mesh=mesh, in_specs=in_specs, out_specs=out_specs, check_vma=False
    )
```

profile of v0, /device:TPU:1, one launch (start us, length us, event | category | flops | bytes accessed | tf_op | source)
XLA Modules:
  0.0 553.9 jit_solution(16415115841045701364)
XLA Ops:
  7.2 5.5 collective-permute-start.1
  12.7 1.3 collective-permute-start
  14.0 1.5 all_to_all.44
  15.5 2.1 copy.16
  17.6 5.3 all-to-all-start.1
  22.8 22.1 %collective-permute-done.1 = f32[96,4,8,128]{3,2,1,0:T(8,128)} collective-permute-done((f32[96,4,8,128]{3,2,1,0:T(8,128)}, f32[96,4,8,128]{3,2,1,0:T(8,128)}, u32[]{:S(2)}, u32[]{:S(2)}) %collective-permute-start.1) | collective-permute-done | bytes 1572896 | tf_op jit(solution)/shard_map/ppermute | solution.py:18
  44.9 2.7 constant_dynamic-update-slice_fusion.3
  47.6 0.0 copy-done
  47.6 2.1 constant_dynamic-update-slice_fusion.1
  49.8 0.1 collective-permute-done
  49.9 11.4 %select_maximum_fusion = f32[96,12,16,136]{3,2,1,0:T(8,128)} fusion(f32[96,4,8,128]{3,2,1,0:T(8,128)} %collective-permute-done, f32[96,4,8,128]{3,2,1,0:T(8,128)S(1)} %copy-done, f32[96,4,8,128]{3,2,1,0:T(8,128)} %collective-permute-done.1), kind=kLoop, calls=%fused_computation.4 | loop fusion | flops 37601280 | bytes 14745600 | tf_op jit(solution)/shard_map/concatenate | solution.py:16
  61.3 2.8 constant_dynamic-update-slice_fusion
  64.0 41.4 %fusion.10 = f32[96,4,8,128]{3,2,1,0:T(8,128)} fusion(f32[96,12,16,136]{3,2,1,0:T(8,128)} %select_maximum_fusion, f32[96,8,8,128]{3,2,1,0:T(8,128)} %get-tuple-element.13, f32[96,8,8,128]{3,2,1,0:T(8,128)} %constant_dynamic-update-slice_fusion, f32[96,4,8,128]{3,2,1,0:T(8,128)S(1)} %copy-done, f32[96,4,8,128]{3,2,1,0:T(8,128)} %collective-permute-done, ...), kind=kLoop, calls=%fused_computation.18 | loop fusion | flops 15728640 | bytes 40910848 | tf_op jit(solution)/shard_map/add | solution.py:55
  105.5 2.6 all_to_all.40
  108.0 3.5 copy.15
  111.5 0.0 all-to-all-done.1
  111.5 6.1 %all-to-all-start = ((f32[96,8,512]{2,0,1:T(8,128)}), f32[96,8,512]{2,0,1:T(8,128)}, u32[]{:S(2)}, u32[]{:S(2)}) async-start(f32[96,8,512]{2,0,1:T(8,128)} %copy.15), calls=%async_computation | async-start | bytes 3145728 | tf_op jit(solution)/shard_map/all_to_all | solution.py:61
  117.6 0.0 all-reduce.5.cloned.1.call-start
  117.6 5.4 fusion.38
  123.0 15.3 %all-to-all-done = f32[96,8,512]{2,0,1:T(8,128)} async-done(((f32[96,8,512]{2,0,1:T(8,128)}), f32[96,8,512]{2,0,1:T(8,128)}, u32[]{:S(2)}, u32[]{:S(2)}) %all-to-all-start) | async-done | bytes 1572896 | tf_op jit(solution)/shard_map/all_to_all | solution.py:61
  138.3 6.8 %convolution_bitcast_fusion = f32[768,768]{1,0:T(8,128)} fusion(f32[768,512]{1,0:T(8,128)} %bitcast.1, f32[768,512]{1,0:T(8,128)S(1)} %bitcast.22), kind=kOutput, calls=%fused_computation.13 | convolution fusion | flops 3623878656 | bytes 5505024 | tf_op jit(solution)/shard_map/dot_general | solution.py:47
  145.1 0.0 all-reduce.5.cloned.1.call-update
  145.1 273.7 %all-reduce.5.cloned.1.call-done = (f32[768,768]{1,0:T(8,128)}, f32[768,768]{1,0:T(8,128)}) async-done(((f32[768,768]{1,0:T(8,128)}, f32[768,768]{1,0:T(8,128)}), (f32[768,768]{1,0:T(8,128)}, f32[768,768]{1,0:T(8,128)})) %all-reduce.5.cloned.1.call-update) | async-done | bytes 4718608 | tf_op jit(solution)/shard_map/psum | solution.py:63
  418.9 5.7 %fusion.3 = f32[768,512]{1,0:T(8,128)S(1)} fusion(f32[768,512]{1,0:T(8,128)S(1)} %bitcast.23, f32[768,768]{1,0:T(8,128)} %get-tuple-element.8), kind=kOutput, calls=%fused_computation.9 | convolution fusion | flops 3624468480 | bytes 5505024 | tf_op jit(solution)/shard_map/dot_general | solution.py:47
  424.6 6.3 %multiply_subtract_fusion = f32[768,512]{1,0:T(8,128)S(1)} fusion(f32[768,512]{1,0:T(8,128)S(1)} %fusion.3, f32[768,512]{1,0:T(8,128)} %bitcast.1, f32[768,768]{1,0:T(8,128)S(1)} %copy-done.1), kind=kOutput, calls=%fused_computation.55 | convolution fusion | flops 3626434560 | bytes 7077888 | tf_op jit(solution)/shard_map/dot_general | solution.py:47
  430.9 27.0 %all_to_all.54 = f32[8,96,512]{2,1,0:T(8,128)S(1)} all-to-all(f32[8,96,512]{2,1,0:T(8,128)S(1)} %bitcast.25), channel_id=1, replica_groups=mesh['orb'=8,'dom'=32] {'orb'}, dimensions={0} | all-to-all | bytes 3145728 | tf_op jit(solution)/shard_map/all_to_all | solution.py:73
  457.9 2.1 copy.18
  459.9 2.4 reshape.24
  462.4 2.9 multiply_reduce_fusion
  465.3 1.0 multiply_reduce_fusion.2
  466.3 74.7 %all-reduce.1 = (f32[]{:T(128)}, f32[]{:T(128)}, f32[]{:T(128)}) all-reduce(f32[]{:T(128)} %multiply_reduce_fusion.2, f32[]{:T(128)} %get-tuple-element.4, f32[]{:T(128)} %get-tuple-element.3), channel_id=1, replica_groups=mesh['orb'=8,'dom'=32] {'orb','dom'}, use_global_device_ids=true, to_apply=%region_3.4 | all-reduce | flops 3 | bytes 24 | tf_op jit(solution)/shard_map/psum | solution.py:75
  542.9 4.1 multiply_add_fusion
  (5 shorter events, 0.0 us)
Async XLA Ops:
  7.2 37.7 %collective-permute-start.1 = (f32[96,4,8,128]{3,2,1,0:T(8,128)}, f32[96,4,8,128]{3,2,1,0:T(8,128)}, u32[]{:S(2)}, u32[]{:S(2)}) collective-permute-start(f32[96,4,8,128]{3,2,1,0:T(8,128)} %param.4), channel_id=1, source_target_pairs={{0,1},{1,2},{2,3},{3,4},{4,5},{5,6},{6,7},{7,8},{8,9},{9,10},{10,1... | collective-permute-start | bytes 4718600 | tf_op jit(solution)/shard_map/ppermute | solution.py:18
  12.7 37.2 %collective-permute-start = (f32[96,4,8,128]{3,2,1,0:T(8,128)}, f32[96,4,8,128]{3,2,1,0:T(8,128)}, u32[]{:S(2)}, u32[]{:S(2)}) collective-permute-start(f32[96,4,8,128]{3,2,1,0:T(8,128)} %param.4), channel_id=1, source_target_pairs={{1,0},{2,1},{3,2},{4,3},{5,4},{6,5},{7,6},{8,7},{9,8},{10,9},{11,1... | collective-permute-start | bytes 4718600 | tf_op jit(solution)/shard_map/ppermute | solution.py:20
  17.6 93.9 %all-to-all-start.1 = ((f32[96,8,512]{2,0,1:T(8,128)}), f32[96,8,512]{2,0,1:T(8,128)S(1)}, u32[]{:S(2)}, u32[]{:S(2)}) async-start(f32[96,8,512]{2,0,1:T(8,128)} %copy.16), calls=%async_computation.1 | async-start | bytes 3145728 | tf_op jit(solution)/shard_map/all_to_all | solution.py:60
  22.8 24.8 %copy-start = (f32[96,4,8,128]{3,2,1,0:T(8,128)S(1)}, f32[96,4,8,128]{3,2,1,0:T(8,128)}, u32[]{:S(2)}) copy-start(f32[96,4,8,128]{3,2,1,0:T(8,128)} %param.4) | copy-start | bytes 4718596
  61.3 2.8 copy-start.2
  111.5 26.8 %all-to-all-start = ((f32[96,8,512]{2,0,1:T(8,128)}), f32[96,8,512]{2,0,1:T(8,128)}, u32[]{:S(2)}, u32[]{:S(2)}) async-start(f32[96,8,512]{2,0,1:T(8,128)} %copy.15), calls=%async_computation | async-start | bytes 3145728 | tf_op jit(solution)/shard_map/all_to_all | solution.py:61
  117.6 301.2 %all-reduce.5.cloned.1.call-start = ((), (), s32[]{:S(2)}) async-start(), calls=%async_computation.3 | async-start | bytes 9437184 | tf_op jit(solution)/shard_map/psum | solution.py:63
  418.9 5.7 %copy-start.1 = (f32[768,768]{1,0:T(8,128)S(1)}, f32[768,768]{1,0:T(8,128)}, u32[]{:S(2)}) copy-start(f32[768,768]{1,0:T(8,128)} %get-tuple-element.9) | copy-start | bytes 7077892
Sparse Core Ops, SparseCore 0:
  145.2 273.5 all-reduce.4
where the time goes:
time: 555 us; the launch traced here: 554 us
  waiting for transfers between devices  311 us (56%)
  blocking collectives  102 us (18%)
  other arithmetic  60.9 us (11%)
  matrix products  24.2 us (4%)
  local copies, waits for them, and re-layouts  21.7 us (4%)
  starting transfers between devices  18.2 us (3%)
  between operations  16 us (3%)
    psum x1, waiting for transfers between devices, on_device(): lax.psum((highdot(cell_orbs, cell_orbs.T), highdot(cell_orbs, cell_images...  274 us
    psum x1, blocking collectives, on_device(): lax.psum((jnp.sum(grad * grad), jnp.sum(grad * prev_gradient), jnp.sum(pr...  74.7 us
    add x1, other arithmetic, on_device(): image = -0.5 * lap + potential[None] * orbitals  41.4 us
    all_to_all x1, blocking collectives, on_device(): lax.all_to_all(cell_grad, 'orb', split_axis=0, concat_axis=1, tiled=True)  27 us
    dot_general x4, matrix products, highdot(): jnp.dot(left, right, precision=lax.Precision.HIGHEST, preferred_element_t...  24.2 us
    ppermute x1, waiting for transfers between devices, padded_2(): lax.ppermute(tail, axis, [(i, (i + 1) % count) for i in range(ends)])  22.1 us
    all_to_all x1, waiting for transfers between devices, on_device(): lax.all_to_all(hmat_rows, 'orb', split_axis=1, concat_axis=0, tiled=True)  15.3 us
    concatenate x1, other arithmetic, padded_2(): jnp.concatenate([lax.ppermute(tail, axis, [(i, (i + 1) % count) for i in...  11.4 us
  transfers between devices with their start and end apart: 5, of which 4 were waited for; matrix products, arithmetic and copies ran while one was open for 13% of the time, Pallas kernels for 0%

commit v1 on v0

--- a/solution.py
+++ b/solution.py
@@ -70,7 +70,10 @@
         - 2.0 * highdot(correlation.T, cell_images)
         - 2.0 * highdot(hamilton.T, cell_orbs)
     )
-    grad = lax.all_to_all(cell_grad, "orb", split_axis=0, concat_axis=1, tiled=True)
+    grad = jnp.concatenate(
+        lax.all_to_all(jnp.stack(jnp.split(cell_grad, lax.axis_size("orb"), axis=0)), "orb", 0, 0),
+        axis=1,
+    )
     grad = grad.reshape(orbitals.shape)
     both, cross, before = lax.psum(
         (

time: 555 us -> 555 us (level)
  no operation moved by 1% of the time
where the time goes in v1:
time: 555 us; the launch traced here: 554 us
  waiting for transfers between devices  311 us (56%)
  blocking collectives  102 us (18%)
  other arithmetic  60.9 us (11%)
  matrix products  24.2 us (4%)
  local copies, waits for them, and re-layouts  21.8 us (4%)
  starting transfers between devices  18.2 us (3%)
  between operations  16.1 us (3%)
    psum x1, waiting for transfers between devices, on_device(): lax.psum((highdot(cell_orbs, cell_orbs.T), highdot(cell_orbs, cell_images...  274 us
    psum x1, blocking collectives, on_device(): lax.psum((jnp.sum(grad * grad), jnp.sum(grad * prev_gradient), jnp.sum(pr...  74.7 us
    add x1, other arithmetic, on_device(): image = -0.5 * lap + potential[None] * orbitals  41.4 us
    all_to_all x1, blocking collectives, on_device(): lax.all_to_all(jnp.stack(jnp.split(cell_grad, lax.axis_size('orb'), axis=...  27 us
    dot_general x4, matrix products, highdot(): jnp.dot(left, right, precision=lax.Precision.HIGHEST, preferred_element_t...  24.2 us
    ppermute x1, waiting for transfers between devices, padded_2(): lax.ppermute(tail, axis, [(i, (i + 1) % count) for i in range(ends)])  22.1 us
    all_to_all x1, waiting for transfers between devices, on_device(): lax.all_to_all(hmat_rows, 'orb', split_axis=1, concat_axis=0, tiled=True)  15.3 us
    concatenate x1, other arithmetic, padded_2(): jnp.concatenate([lax.ppermute(tail, axis, [(i, (i + 1) % count) for i in...  11.4 us
  transfers between devices with their start and end apart: 5, of which 4 were waited for; matrix products, arithmetic and copies ran while one was open for 13% of the time, Pallas kernels for 0%

profile of v1, /device:TPU:1, one launch (start us, length us, event | category | flops | bytes accessed | tf_op | source)
XLA Modules:
  0.0 554.1 jit_solution(9070393580727904230)
XLA Ops:
  7.2 5.5 collective-permute-start.1
  12.7 1.3 collective-permute-start
  14.0 1.5 all_to_all.35
  15.5 2.1 copy.15
  17.6 5.3 all-to-all-start.1
  22.8 22.1 %collective-permute-done.1 = f32[96,4,8,128]{3,2,1,0:T(8,128)} collective-permute-done((f32[96,4,8,128]{3,2,1,0:T(8,128)}, f32[96,4,8,128]{3,2,1,0:T(8,128)}, u32[]{:S(2)}, u32[]{:S(2)}) %collective-permute-start.1) | collective-permute-done | bytes 1572896 | tf_op jit(solution)/shard_map/ppermute | solution.py:18
  44.9 2.7 constant_dynamic-update-slice_fusion.3
  47.6 0.0 copy-done
  47.6 2.1 constant_dynamic-update-slice_fusion.1
  49.8 0.1 collective-permute-done
  49.9 11.4 %select_maximum_fusion = f32[96,12,16,136]{3,2,1,0:T(8,128)} fusion(f32[96,4,8,128]{3,2,1,0:T(8,128)} %collective-permute-done, f32[96,4,8,128]{3,2,1,0:T(8,128)S(1)} %copy-done, f32[96,4,8,128]{3,2,1,0:T(8,128)} %collective-permute-done.1), kind=kLoop, calls=%fused_computation.4 | loop fusion | flops 37601280 | bytes 14745600 | tf_op jit(solution)/shard_map/concatenate | solution.py:16
  61.3 2.8 constant_dynamic-update-slice_fusion
  64.0 41.4 %fusion.10 = f32[96,4,8,128]{3,2,1,0:T(8,128)} fusion(f32[96,12,16,136]{3,2,1,0:T(8,128)} %select_maximum_fusion, f32[96,8,8,128]{3,2,1,0:T(8,128)} %get-tuple-element.13, f32[96,8,8,128]{3,2,1,0:T(8,128)} %constant_dynamic-update-slice_fusion, f32[96,4,8,128]{3,2,1,0:T(8,128)S(1)} %copy-done, f32[96,4,8,128]{3,2,1,0:T(8,128)} %collective-permute-done, ...), kind=kLoop, calls=%fused_computation.18 | loop fusion | flops 15728640 | bytes 40910848 | tf_op jit(solution)/shard_map/add | solution.py:55
  105.5 2.6 all_to_all.31
  108.0 3.5 copy.14
  111.5 0.0 all-to-all-done.1
  111.5 6.1 %all-to-all-start = ((f32[96,8,512]{2,0,1:T(8,128)}), f32[96,8,512]{2,0,1:T(8,128)}, u32[]{:S(2)}, u32[]{:S(2)}) async-start(f32[96,8,512]{2,0,1:T(8,128)} %copy.14), calls=%async_computation | async-start | bytes 3145728 | tf_op jit(solution)/shard_map/all_to_all | solution.py:61
  117.6 0.0 all-reduce.5.cloned.1.call-start
  117.6 5.4 fusion.46
  123.0 15.3 %all-to-all-done = f32[96,8,512]{2,0,1:T(8,128)} async-done(((f32[96,8,512]{2,0,1:T(8,128)}), f32[96,8,512]{2,0,1:T(8,128)}, u32[]{:S(2)}, u32[]{:S(2)}) %all-to-all-start) | async-done | bytes 1572896 | tf_op jit(solution)/shard_map/all_to_all | solution.py:61
  138.3 6.8 %convolution_bitcast_fusion = f32[768,768]{1,0:T(8,128)} fusion(f32[768,512]{1,0:T(8,128)} %bitcast.1, f32[768,512]{1,0:T(8,128)S(1)} %bitcast.53), kind=kOutput, calls=%fused_computation.13 | convolution fusion | flops 3623878656 | bytes 5505024 | tf_op jit(solution)/shard_map/dot_general | solution.py:47
  145.1 0.0 all-reduce.5.cloned.1.call-update
  145.1 273.7 %all-reduce.5.cloned.1.call-done = (f32[768,768]{1,0:T(8,128)}, f32[768,768]{1,0:T(8,128)}) async-done(((f32[768,768]{1,0:T(8,128)}, f32[768,768]{1,0:T(8,128)}), (f32[768,768]{1,0:T(8,128)}, f32[768,768]{1,0:T(8,128)})) %all-reduce.5.cloned.1.call-update) | async-done | bytes 4718608 | tf_op jit(solution)/shard_map/psum | solution.py:63
  418.9 5.7 %fusion.3 = f32[768,512]{1,0:T(8,128)S(1)} fusion(f32[768,512]{1,0:T(8,128)S(1)} %bitcast.54, f32[768,768]{1,0:T(8,128)} %get-tuple-element.8), kind=kOutput, calls=%fused_computation.9 | convolution fusion | flops 3624468480 | bytes 5505024 | tf_op jit(solution)/shard_map/dot_general | solution.py:47
  424.6 6.3 %multiply_subtract_fusion = f32[768,512]{1,0:T(8,128)S(1)} fusion(f32[768,512]{1,0:T(8,128)S(1)} %fusion.3, f32[768,512]{1,0:T(8,128)} %bitcast.1, f32[768,768]{1,0:T(8,128)S(1)} %copy-done.1), kind=kOutput, calls=%fused_computation.55 | convolution fusion | flops 3626434560 | bytes 7077888 | tf_op jit(solution)/shard_map/dot_general | solution.py:47
  431.1 27.0 %all_to_all.43 = f32[8,96,512]{2,1,0:T(8,128)S(1)} all-to-all(f32[8,96,512]{2,1,0:T(8,128)S(1)} %fusion.36), channel_id=1, replica_groups=mesh['orb'=8,'dom'=32] {'orb'}, dimensions={0} | all-to-all | bytes 3145728 | tf_op jit(solution)/shard_map/all_to_all | solution.py:74
  458.0 2.1 copy.17
  460.1 2.4 reshape_reshape.3
  462.5 2.9 multiply_reduce_fusion
  465.5 1.0 multiply_reduce_fusion.2
  466.5 74.7 %all-reduce.1 = (f32[]{:T(128)}, f32[]{:T(128)}, f32[]{:T(128)}) all-reduce(f32[]{:T(128)} %multiply_reduce_fusion.2, f32[]{:T(128)} %get-tuple-element.4, f32[]{:T(128)} %get-tuple-element.3), channel_id=1, replica_groups=mesh['orb'=8,'dom'=32] {'orb','dom'}, use_global_device_ids=true, to_apply=%region_3.4 | all-reduce | flops 3 | bytes 24 | tf_op jit(solution)/shard_map/psum | solution.py:78
  543.1 4.1 multiply_add_fusion
  (13 shorter events, 0.1 us)
Async XLA Ops:
  7.2 37.7 %collective-permute-start.1 = (f32[96,4,8,128]{3,2,1,0:T(8,128)}, f32[96,4,8,128]{3,2,1,0:T(8,128)}, u32[]{:S(2)}, u32[]{:S(2)}) collective-permute-start(f32[96,4,8,128]{3,2,1,0:T(8,128)} %param.4), channel_id=1, source_target_pairs={{0,1},{1,2},{2,3},{3,4},{4,5},{5,6},{6,7},{7,8},{8,9},{9,10},{10,1... | collective-permute-start | bytes 4718600 | tf_op jit(solution)/shard_map/ppermute | solution.py:18
  12.7 37.2 %collective-permute-start = (f32[96,4,8,128]{3,2,1,0:T(8,128)}, f32[96,4,8,128]{3,2,1,0:T(8,128)}, u32[]{:S(2)}, u32[]{:S(2)}) collective-permute-start(f32[96,4,8,128]{3,2,1,0:T(8,128)} %param.4), channel_id=1, source_target_pairs={{1,0},{2,1},{3,2},{4,3},{5,4},{6,5},{7,6},{8,7},{9,8},{10,9},{11,1... | collective-permute-start | bytes 4718600 | tf_op jit(solution)/shard_map/ppermute | solution.py:20
  17.6 93.9 %all-to-all-start.1 = ((f32[96,8,512]{2,0,1:T(8,128)}), f32[96,8,512]{2,0,1:T(8,128)S(1)}, u32[]{:S(2)}, u32[]{:S(2)}) async-start(f32[96,8,512]{2,0,1:T(8,128)} %copy.15), calls=%async_computation.1 | async-start | bytes 3145728 | tf_op jit(solution)/shard_map/all_to_all | solution.py:60
  22.8 24.8 %copy-start = (f32[96,4,8,128]{3,2,1,0:T(8,128)S(1)}, f32[96,4,8,128]{3,2,1,0:T(8,128)}, u32[]{:S(2)}) copy-start(f32[96,4,8,128]{3,2,1,0:T(8,128)} %param.4) | copy-start | bytes 4718596
  61.3 2.8 copy-start.2
  111.5 26.8 %all-to-all-start = ((f32[96,8,512]{2,0,1:T(8,128)}), f32[96,8,512]{2,0,1:T(8,128)}, u32[]{:S(2)}, u32[]{:S(2)}) async-start(f32[96,8,512]{2,0,1:T(8,128)} %copy.14), calls=%async_computation | async-start | bytes 3145728 | tf_op jit(solution)/shard_map/all_to_all | solution.py:61
  117.6 301.2 %all-reduce.5.cloned.1.call-start = ((), (), s32[]{:S(2)}) async-start(), calls=%async_computation.3 | async-start | bytes 9437184 | tf_op jit(solution)/shard_map/psum | solution.py:63
  418.9 5.7 %copy-start.1 = (f32[768,768]{1,0:T(8,128)S(1)}, f32[768,768]{1,0:T(8,128)}, u32[]{:S(2)}) copy-start(f32[768,768]{1,0:T(8,128)} %get-tuple-element.9) | copy-start | bytes 7077892
Sparse Core Ops, SparseCore 0:
  145.2 273.5 all-reduce.4
